TPU v7x, 512 devices: a whole 4x4x16 slice. The times are simulated.
512 devices in a mesh: tm: 32 (over z, x_lo), height: 16 (over y, x_hi, core).
Axes of the slice: x: 4 (x_hi: 2, x_lo: 2; x = x_hi * 2 + x_lo), y: 4, z: 16, core: 2. Of those that a mesh axis runs over, the one named last changes fastest.
Arguments:
- frames_in: bfloat16 [512, 128, 1024], P('tm', 'height'), may hold values from -6 to 6
- time_filter: bfloat16 [512, 64], replicated, may hold values from -0.25 to 0.25
- height_filter: bfloat16 [128, 64], replicated, may hold values from -0.5 to 0.5
Outputs:
- layer_out: bfloat16 [512, 128, 1024], P('tm', 'height')
All inputs are finite; a program needn't handle non-finite values.
Results may differ from a plain program's by a relative error of at most 0.0051.
Values may be sent and summed in bfloat16 or wider, within the bound.
A program may use at most 64 MiB of HBM per device.

v0:
```python
import jax
import jax.numpy as jnp
from jax import lax
from jax.sharding import PartitionSpec as P


def lane_taps(tap_table, first_lane, lane_count):
    channels = tap_table.shape[1]
    distinct = min(lane_count, channels)
    lane_ids = (first_lane + lax.iota(jnp.int32, distinct)) % channels
    selector = (lane_ids[None, :] == lax.iota(jnp.int32, channels)[:, None]).astype(tap_table.dtype)
    picked = jnp.dot(tap_table, selector, preferred_element_type=jnp.float32).astype(
        tap_table.dtype
    )
    return jnp.transpose(picked)


def shifted_taps(taps, base, size):
    distinct, period = taps.shape
    start = (base - (size - 1)) % period
    tiled = jnp.concatenate([taps, taps, taps], axis=1)
    window = lax.slice_in_dim(tiled, start, start + 2 * size - 1, axis=1)
    reversed_window = window[:, ::-1]
    padded = jnp.concatenate([reversed_window, jnp.zeros((distinct, 1), taps.dtype)], axis=1)
    repeated = jnp.tile(padded, (1, size + 1))
    flat = lax.slice_in_dim(repeated, size - 1, size - 1 + size * (2 * size - 1), axis=1)
    return flat.reshape(distinct, size, 2 * size - 1)[:, :, :size]


def time_convolve(segment, own_taps):
    frames, rows_here, lane_count = segment.shape
    distinct = own_taps.shape[0]
    columns = lane_count // distinct
    block_len = min(128, frames)
    block_count = frames // block_len
    blocked = segment.reshape(block_count, block_len, rows_here, columns, distinct)
    blocked = jnp.transpose(blocked, (4, 3, 2, 0, 1))
    running = jnp.zeros((distinct, columns, rows_here, block_count, block_len), jnp.float32)
    for lag_index in range(block_count):
        toeplitz = shifted_taps(own_taps, lag_index * block_len, block_len)
        rolled = jnp.roll(blocked, lag_index, axis=3)
        running = running + jnp.einsum(
            "cab,cxrnb->cxrna", toeplitz, rolled, preferred_element_type=jnp.float32
        )
    result = jnp.transpose(running, (3, 4, 2, 1, 0)).reshape(frames, rows_here, lane_count)
    return result.astype(jnp.bfloat16)


def row_convolve(segment, row_taps):
    frames, height, lane_count = segment.shape
    distinct = row_taps.shape[0]
    columns = lane_count // distinct
    arranged = jnp.transpose(segment.reshape(frames, height, columns, distinct), (3, 2, 0, 1))
    circulant = shifted_taps(row_taps, 0, height)
    filtered = jnp.einsum("cab,cxfb->cxfa", circulant, arranged, preferred_element_type=jnp.float32)
    result = jnp.transpose(filtered, (2, 3, 1, 0)).reshape(frames, height, lane_count)
    return result.astype(jnp.bfloat16)


def shards(frames_in, time_filter, height_filter):
    frames_dev, rows_dev, lane_total = frames_in.shape
    tm_count = lax.axis_size("tm")
    height_count = lax.axis_size("height")
    lane_count = lane_total // tm_count
    own_taps = lane_taps(time_filter, lax.axis_index("tm") * lane_count, lane_count)
    result = time_convolve(
        lax.all_to_all(frames_in, "tm", split_axis=2, concat_axis=0, tiled=True), own_taps
    )
    temporal = lax.all_to_all(result, "tm", split_axis=0, concat_axis=2, tiled=True)
    slice_width = lane_total // height_count
    row_taps = lane_taps(height_filter, lax.axis_index("height") * slice_width, slice_width)
    result = row_convolve(
        lax.all_to_all(temporal, "height", split_axis=2, concat_axis=1, tiled=True), row_taps
    )
    spatial = lax.all_to_all(result, "height", split_axis=1, concat_axis=2, tiled=True)
    return (frames_in.astype(jnp.float32) + spatial.astype(jnp.float32)).astype(jnp.bfloat16)


def solution(mesh):
    return jax.shard_map(
        shards,
        mesh=mesh,
        in_specs=(P("tm", "height", None), P(), P()),
        out_specs=P("tm", "height", None),
        check_vma=False,
    )
```

profile of v0, /device:TPU:1, one launch (start us, length us, event | category | flops | bytes accessed | tf_op | source)
XLA Modules:
  0.0 163.0 jit_solution(17824407063810150623)
XLA Ops:
  0.0 2.7 %copy.34 = bf16[16,8,1024]{0,1,2:T(8,128)(2,1)S(1)} copy(bf16[16,8,1024]{2,1,0:T(8,128)(2,1)} %param.3) | data formatting | bytes 524288 | tf_op args[0]
  2.7 2.9 %reshape.124 = bf16[32,2,2048]{2,1,0:T(2,128)(2,1)} reshape(bf16[1024,8,16]{2,1,0:T(8,128)(2,1)S(1)} %bitcast.104) | data formatting | bytes 524288
  5.6 17.1 %all-to-all-start = ((bf16[32,2,2048]{2,1,0:T(2,128)(2,1)}), bf16[32,2,2048]{2,1,0:T(2,128)(2,1)S(1)}, u32[]{:S(2)}, u32[]{:S(2)}) async-start(bf16[32,2,2048]{2,1,0:T(2,128)(2,1)} %reshape.124), calls=%async_computation | async-start | bytes 524288 | tf_op jit(solution)/shard_map/all_to_all | solution.py:67
  25.3 7.8 %reshape.106 = bf16[32,128,255]{2,1,0:T(8,128)(2,1)} reshape(bf16[32,32640]{1,0:T(8,128)(2,1)S(1)} %slice.90) | data formatting | bytes 4177920 | tf_op jit(solution)/shard_map/reshape | solution.py:27
  34.3 7.8 %reshape.110 = bf16[32,128,255]{2,1,0:T(8,128)(2,1)} reshape(bf16[32,32640]{1,0:T(8,128)(2,1)S(1)} %slice.95) | data formatting | bytes 4177920 | tf_op jit(solution)/shard_map/reshape | solution.py:27
  43.3 7.8 %reshape.112 = bf16[32,128,255]{2,1,0:T(8,128)(2,1)} reshape(bf16[32,32640]{1,0:T(8,128)(2,1)S(1)} %slice.100) | data formatting | bytes 4177920 | tf_op jit(solution)/shard_map/reshape | solution.py:27
  52.3 7.8 %reshape.114 = bf16[32,128,255]{2,1,0:T(8,128)(2,1)} reshape(bf16[32,32640]{1,0:T(8,128)(2,1)S(1)} %slice.105) | data formatting | bytes 4177920 | tf_op jit(solution)/shard_map/reshape | solution.py:27
  60.1 1.4 reshape.125
  61.5 1.4 copy.35
  63.0 0.9 copy.36
  68.7 1.7 %reshape.126 = bf16[32,2,2048]{2,1,0:T(2,128)(2,1)} reshape(bf16[512,8,32]{2,1,0:T(8,128)(2,1)S(1)} %bitcast.114) | data formatting | bytes 524288
  70.4 12.3 %all-to-all-start.1 = ((bf16[32,2,2048]{2,1,0:T(2,128)(2,1)}), bf16[32,2,2048]{2,1,0:T(2,128)(2,1)S(1)}, u32[]{:S(2)}, u32[]{:S(2)}) async-start(bf16[32,2,2048]{2,1,0:T(2,128)(2,1)} %reshape.126), calls=%async_computation.1 | async-start | bytes 524288 | tf_op jit(solution)/shard_map/all_to_all | solution.py:69
  82.8 19.8 %all-to-all-done.1 = bf16[32,2,2048]{2,1,0:T(2,128)(2,1)S(1)} async-done(((bf16[32,2,2048]{2,1,0:T(2,128)(2,1)}), bf16[32,2,2048]{2,1,0:T(2,128)(2,1)S(1)}, u32[]{:S(2)}, u32[]{:S(2)}) %all-to-all-start.1) | async-done | bytes 262176 | tf_op jit(solution)/shard_map/all_to_all | solution.py:69
  103.1 1.5 copy.52
  104.6 2.8 %reshape.128 = bf16[16,2,4096]{2,1,0:T(2,128)(2,1)} reshape(bf16[1024,8,16]{2,1,0:T(8,128)(2,1)S(1)} %bitcast.103) | data formatting | bytes 524288
  107.4 9.7 %all-to-all-start.2 = ((bf16[16,2,4096]{2,1,0:T(2,128)(2,1)}), bf16[16,2,4096]{2,1,0:T(2,128)(2,1)S(1)}, u32[]{:S(2)}, u32[]{:S(2)}) async-start(bf16[16,2,4096]{2,1,0:T(2,128)(2,1)} %reshape.128), calls=%async_computation.2 | async-start | bytes 524288 | tf_op jit(solution)/shard_map/all_to_all | solution.py:73
  117.9 0.9 copy.61
  118.9 3.2 %slice.107 = bf16[64,32640]{1,0:T(8,128)(2,1)} slice(bf16[64,33024]{1,0:T(8,128)(2,1)S(1)} %bitcast.96), slice={[0:64], [127:32767]} | slice | bytes 8355840 | tf_op jit(solution)/shard_map/slice | solution.py:26
  122.1 15.9 %reshape.117 = bf16[64,128,255]{2,1,0:T(8,128)(2,1)} reshape(bf16[64,32640]{1,0:T(8,128)(2,1)} %slice.107) | data formatting | bytes 8355840 | tf_op jit(solution)/shard_map/reshape | solution.py:27
  137.9 1.4 reshape.129
  139.4 1.7 %copy.42 = bf16[16,16,8,64]{3,2,1,0:T(8,128)(2,1)S(1)} copy(bf16[16,16,8,64]{0,2,3,1:T(8,128)(2,1)S(1)} %bitcast.101) | data formatting | bytes 524288 | tf_op jit(solution)/shard_map/all_to_all | solution.py:73
  141.3 2.8 %fusion.6 = bf16[16,128,64]{1,0,2:T(8,128)(2,1)S(1)} fusion(bf16[64,128,255]{2,1,0:T(8,128)(2,1)} %reshape.117, bf16[16,128,1,64]{1,0,3,2:T(8,128)(2,1)S(1)} %copy.43), kind=kOutput, calls=%fused_computation.8 | convolution fusion | flops 33685504 | bytes 2621440 | tf_op jit(solution)/shard_map/cab,cxfb->cxfa/dot_general | solution.py:55
  145.0 15.7 %all_to_all.57 = bf16[16,2,4096]{2,1,0:T(2,128)(2,1)S(1)} all-to-all(bf16[16,2,4096]{2,1,0:T(2,128)(2,1)S(1)} %reshape.130), channel_id=1, replica_groups=mesh['tm'=32,'height'=16] {'height'}, dimensions={0} | all-to-all | bytes 524288 | tf_op jit(solution)/shard_map/all_to_all | solution.py:75
  162.2 0.8 add_convert_fusion
  (68 shorter events, 14.9 us)
Async XLA Ops:
  0.0 22.7 %copy-start = (bf16[512,64]{0,1:T(8,128)(2,1)S(1)}, bf16[512,64]{0,1:T(8,128)(2,1)}, u32[]{:S(2)}) copy-start(bf16[512,64]{0,1:T(8,128)(2,1)} %param.4) | copy-start | bytes 196612
  5.6 54.5 %all-to-all-start = ((bf16[32,2,2048]{2,1,0:T(2,128)(2,1)}), bf16[32,2,2048]{2,1,0:T(2,128)(2,1)S(1)}, u32[]{:S(2)}, u32[]{:S(2)}) async-start(bf16[32,2,2048]{2,1,0:T(2,128)(2,1)} %reshape.124), calls=%async_computation | async-start | bytes 524288 | tf_op jit(solution)/shard_map/all_to_all | solution.py:67
  63.0 1.6 copy-start.2
  63.9 1.8 %copy-start.3 = (bf16[32,128,255]{2,1,0:T(8,128)(2,1)S(1)}, bf16[32,128,255]{2,1,0:T(8,128)(2,1)}, u32[]{:S(2)}) copy-start(bf16[32,128,255]{2,1,0:T(8,128)(2,1)} %reshape.110) | copy-start | bytes 6266884
  64.6 1.7 %copy-start.4 = (bf16[32,128,255]{2,1,0:T(8,128)(2,1)S(1)}, bf16[32,128,255]{2,1,0:T(8,128)(2,1)}, u32[]{:S(2)}) copy-start(bf16[32,128,255]{2,1,0:T(8,128)(2,1)} %reshape.112) | copy-start | bytes 6266884
  65.6 1.7 %copy-start.5 = (bf16[32,128,255]{2,1,0:T(8,128)(2,1)S(1)}, bf16[32,128,255]{2,1,0:T(8,128)(2,1)}, u32[]{:S(2)}) copy-start(bf16[32,128,255]{2,1,0:T(8,128)(2,1)} %reshape.114) | copy-start | bytes 6266884
  70.4 32.2 %all-to-all-start.1 = ((bf16[32,2,2048]{2,1,0:T(2,128)(2,1)}), bf16[32,2,2048]{2,1,0:T(2,128)(2,1)S(1)}, u32[]{:S(2)}, u32[]{:S(2)}) async-start(bf16[32,2,2048]{2,1,0:T(2,128)(2,1)} %reshape.126), calls=%async_computation.1 | async-start | bytes 524288 | tf_op jit(solution)/shard_map/all_to_all | solution.py:69
  104.6 12.5 %copy-start.7 = (bf16[128,64]{0,1:T(8,128)(2,1)S(1)}, bf16[128,64]{0,1:T(8,128)(2,1)}, u32[]{:S(2)}) copy-start(bf16[128,64]{0,1:T(8,128)(2,1)} %param.5) | copy-start | bytes 49156
  107.4 30.6 %all-to-all-start.2 = ((bf16[16,2,4096]{2,1,0:T(2,128)(2,1)}), bf16[16,2,4096]{2,1,0:T(2,128)(2,1)S(1)}, u32[]{:S(2)}, u32[]{:S(2)}) async-start(bf16[16,2,4096]{2,1,0:T(2,128)(2,1)} %reshape.128), calls=%async_computation.2 | async-start | bytes 524288 | tf_op jit(solution)/shard_map/all_to_all | solution.py:73
  161.1 1.9 %copy-start.1 = (bf16[512,64]{0,1:T(8,128)(2,1)S(1)}, bf16[512,64]{0,1:T(8,128)(2,1)}, u32[]{:S(2)}) copy-start(bf16[512,64]{0,1:T(8,128)(2,1)} %param.4) | copy-start | bytes 196612
  161.2 1.0 copy-start.6
where the time goes:
time: 163 us
  local copies, waits for them, and re-layouts  81.2 us (50%)
  starting transfers between devices  39.2 us (24%)
  waiting for transfers between devices  19.8 us (12%)
  blocking collectives  15.7 us (10%)
  matrix products  5.71 us (4%)
    reshape x5, local copies, waits for them, and re-layouts, shifted_taps(): return flat.reshape(distinct, size, 2 * size - 1)[:, :, :size]  47.1 us
    unnamed x40, local copies, waits for them, and re-layouts  19.9 us
    all_to_all x1, waiting for transfers between devices, shards(): lax.all_to_all(result, 'tm', split_axis=0, concat_axis=2, tiled=True)  19.8 us
    all_to_all x1, starting transfers between devices, shards(): lax.all_to_all(frames_in, 'tm', split_axis=2, concat_axis=0, tiled=True)  17.1 us
    all_to_all x1, blocking collectives, shards(): lax.all_to_all(result, 'height', split_axis=1, concat_axis=2, tiled=True)  15.7 us
    all_to_all x1, starting transfers between devices, shards(): lax.all_to_all(result, 'tm', split_axis=0, concat_axis=2, tiled=True)  12.3 us
    all_to_all x1, starting transfers between devices, shards(): lax.all_to_all(temporal, 'height', split_axis=2, concat_axis=1, tiled=True)  9.68 us
    slice x5, local copies, waits for them, and re-layouts, shifted_taps(): lax.slice_in_dim(repeated, size - 1, size - 1 + size * (2 * size - 1), ax...  5.65 us
  transfers between devices with their start and end apart: 3, of which 1 were waited for; matrix products, arithmetic and copies ran while one was open for 36% of the time, Pallas kernels for 0%

commit v1 on v0

v1 whole, which is shorter than its diff:
```python
import functools

import jax
import jax.numpy as jnp
import numpy as np
from jax import lax
from jax.experimental import pallas as pl
from jax.experimental.pallas import tpu as pltpu
from jax.sharding import PartitionSpec as P

MESH = pl.DeviceIdType.MESH
F32, BF16 = jnp.float32, jnp.bfloat16
LANE = 128
CHUNKS = 2


def dft_tables(size):
    half = size // 2
    angle = 2.0 * np.pi * ((np.arange(half)[:, None] * np.arange(size)[None, :]) % size) / size
    sines = np.sin(angle)
    sines[0] = np.cos(np.pi * np.arange(size))
    table = np.concatenate([np.cos(angle), sines], axis=0)
    high = table.astype(np.float32).astype(jnp.bfloat16)
    low = (table - high.astype(np.float64)).astype(np.float32).astype(jnp.bfloat16)
    forward = np.concatenate([high, low], axis=0)
    inverse = np.stack([high.T, low.T])
    return forward, inverse


def dot(a, b):
    return jnp.dot(a, b, preferred_element_type=F32)


def one_hot(shape, hit):
    rows = lax.broadcasted_iota(jnp.int32, shape, 0)
    cols = lax.broadcasted_iota(jnp.int32, shape, 1)
    return jnp.where(hit(rows, cols), 1.0, 0.0).astype(BF16)


def forward_dft(forward, values):
    size = values.shape[0]
    both = dot(forward[...], values)
    return both[:size] + both[size:]


def inverse_dft(inverse, spectrum):
    lanes = spectrum.shape[1]
    high = spectrum.astype(BF16)
    low = (spectrum - high.astype(F32)).astype(BF16)
    main = dot(inverse[0], jnp.concatenate([high, low], axis=1))
    return main[:, :lanes] + main[:, lanes:] + dot(inverse[1], high)


def store_response(forward, taps, response):
    size, channels = taps.shape
    half = size // 2
    spread = one_hot((channels, LANE), lambda r, c: r == c % channels)
    spectrum = forward_dft(forward, dot(taps[...], spread).astype(BF16))
    first = lax.broadcasted_iota(jnp.int32, (half, LANE), 0) == 0
    scale = jnp.where(first, 1.0 / size, 2.0 / size)
    cosine, sine = spectrum[:half] * scale, spectrum[half:] * scale
    response[0] = cosine
    response[1] = jnp.where(first, 0.0, sine)
    response[2] = jnp.where(first, sine, cosine)


def filtered(forward, inverse, response, values):
    size, lanes = values.shape
    half = size // 2
    spectrum = forward_dft(forward, values)
    cosine, sine = spectrum[:half], spectrum[half:]
    wide = lambda which: jnp.concatenate([response[which]] * (lanes // LANE), axis=1)
    p, q, nyquist_p = wide(0), wide(1), wide(2)
    product = jnp.concatenate([cosine * p - sine * q, cosine * q + sine * nyquist_p], axis=0)
    return inverse_dft(inverse, product)


def kernel(
    tm_count, height_count,
    frames_hbm, time_taps, height_taps, tf_hbm, ti_hbm, hf_hbm, hi_hbm,
    out,
    frames, tf, ti, hf, hi, t_response, h_response,
    t_send, t_have, t_done, t_back, h_send, h_have, h_done, h_back,
    load_sems, own_sems, send_sems, recv_sems,
):
    frames_dev, rows_dev, lane_total = frames.shape
    width = lane_total // CHUNKS
    groups = width // LANE
    block = frames_dev * rows_dev
    tm = lax.axis_index("tm")
    height = lax.axis_index("height")
    z, x_lo = tm // 2, tm % 2
    z_count = tm_count // 2

    loads = [
        pltpu.make_async_copy(src, dst, load_sems.at[i])
        for i, (src, dst) in enumerate(
            [(frames_hbm, frames), (tf_hbm, tf), (ti_hbm, ti), (hf_hbm, hf), (hi_hbm, hi)]
        )
    ]
    for load in loads:
        load.start()

    barrier = pltpu.get_barrier_semaphore()

    def greet_tm(d, carry):
        peer = (tm + d) % tm_count
        pl.semaphore_signal(barrier, inc=1, device_id=(peer, height), device_id_type=MESH)
        return carry

    def greet_height(d, carry):
        peer = (height + d) % height_count
        pl.semaphore_signal(barrier, inc=1, device_id=(tm, peer), device_id_type=MESH)
        return carry

    lax.fori_loop(1, tm_count, greet_tm, 0)
    lax.fori_loop(1, height_count, greet_height, 0)

    loads[0].wait()
    swap_in = one_hot((block, block), lambda r, c: c == (r % frames_dev) * rows_dev + r // frames_dev)
    rows = frames[...].astype(F32).reshape(block, lane_total).astype(BF16)
    turned = dot(swap_in, rows).astype(BF16)
    for c in range(CHUNKS):
        for g in range(groups):
            lo = c * width + g * LANE
            t_send[c, g * rows_dev:(g + 1) * rows_dev] = turned[:, lo:lo + LANE].reshape(
                rows_dev, frames_dev, LANE
            )

    pl.semaphore_wait(barrier, tm_count + height_count - 2)

    def tm_peer(i):
        k = i // 2
        away = z_count // 2 + ((k + 1) // 2) * (1 - 2 * (k % 2))
        return ((z + away) % z_count) * 2 + (x_lo + 1 - i % 2) % 2

    def exchange_tm(phase, c, src, dst):
        pltpu.make_async_copy(src.at[c, tm], dst.at[c, tm], recv_sems.at[phase, c]).start()

        def send(i, carry):
            peer = tm_peer(i)
            pltpu.make_async_remote_copy(
                src_ref=src.at[c, peer], dst_ref=dst.at[c, tm],
                send_sem=send_sems.at[phase, c], recv_sem=recv_sems.at[phase, c],
                device_id=(peer, height), device_id_type=MESH,
            ).start()
            return carry

        lax.fori_loop(0, tm_count - 1, send, 0)

    def exchange_height(phase, c, src, dst):
        pltpu.make_async_copy(src.at[c, height], dst.at[c, height], recv_sems.at[phase, c]).start()

        def send(d, carry):
            peer = (height + d) % height_count
            pltpu.make_async_remote_copy(
                src_ref=src.at[c, peer], dst_ref=dst.at[c, height],
                send_sem=send_sems.at[phase, c], recv_sem=recv_sems.at[phase, c],
                device_id=(tm, peer), device_id_type=MESH,
            ).start()
            return carry

        lax.fori_loop(1, height_count, send, 0)

    def arrived(phase, c, dst):
        pltpu.make_async_copy(dst.at[c], dst.at[c], recv_sems.at[phase, c]).wait()

    def departed(phase, c, src, peers):
        sent = src.at[c, pl.ds(0, peers - 1)]
        pltpu.make_async_copy(sent, sent, send_sems.at[phase, c]).wait()

    for c in range(CHUNKS):
        exchange_tm(0, c, t_send, t_have)

    for load in loads[1:]:
        load.wait()
    store_response(tf, time_taps, t_response)
    store_response(hf, height_taps, h_response)

    def time_stage(c, carry):
        arrived(0, c, t_have)
        values = t_have[c].reshape(tm_count * frames_dev, LANE)
        result = filtered(tf, ti, t_response, values).astype(BF16)
        t_done[c] = result.reshape(tm_count, frames_dev, LANE)
        exchange_tm(1, c, t_done, t_back)
        return carry

    lax.fori_loop(0, CHUNKS, time_stage, 0)

    swap_back = one_hot((block, block), lambda r, c: c == (r % rows_dev) * frames_dev + r // rows_dev)

    def height_stage(c, carry):
        arrived(1, c, t_back)
        for g in range(groups):
            tile = t_back[c, g * rows_dev:(g + 1) * rows_dev].reshape(block, LANE)
            turned = dot(swap_back, tile).reshape(frames_dev, rows_dev, LANE)
            h_send[c, :, :, g * LANE:(g + 1) * LANE] = turned.astype(BF16)
        exchange_height(2, c, h_send, h_have)
        arrived(2, c, h_have)
        values = h_have[c].astype(F32).reshape(height_count * rows_dev, width).astype(BF16)
        result = filtered(hf, hi, h_response, values)
        h_done[c] = result.reshape(height_count, rows_dev, width).astype(BF16)
        exchange_height(3, c, h_done, h_back)
        return carry

    lax.fori_loop(0, CHUNKS, height_stage, 0)

    for c in range(CHUNKS):
        arrived(3, c, h_back)
        lanes = slice(c * width, (c + 1) * width)
        total = frames[:, :, lanes].astype(F32) + h_back[c].astype(F32)
        out[:, :, lanes] = total.astype(BF16)

    for c in range(CHUNKS):
        departed(0, c, t_send, tm_count)
        departed(1, c, t_done, tm_count)
        departed(2, c, h_send, height_count)
        departed(3, c, h_done, height_count)


def shards(frames_in, time_filter, height_filter):
    frames_dev, rows_dev, lane_total = frames_in.shape
    tm_count = lax.axis_size("tm")
    height_count = lax.axis_size("height")
    width = lane_total // CHUNKS
    tf, ti = dft_tables(time_filter.shape[0])
    hf, hi = dft_tables(height_filter.shape[0])
    t_buf = pltpu.VMEM((CHUNKS, tm_count, frames_dev, LANE), BF16)
    h_buf = pltpu.VMEM((CHUNKS, height_count, rows_dev, width), BF16)
    like = lambda a: pltpu.VMEM(a.shape, BF16)
    hbm = pl.BlockSpec(memory_space=pl.ANY)
    vmem = pl.BlockSpec(memory_space=pltpu.VMEM)
    return pl.pallas_call(
        functools.partial(kernel, tm_count, height_count),
        out_shape=jax.ShapeDtypeStruct(frames_in.shape, BF16),
        in_specs=[hbm, vmem, vmem, hbm, hbm, hbm, hbm],
        out_specs=vmem,
        scratch_shapes=[
            pltpu.VMEM(frames_in.shape, BF16),
            like(tf), like(ti), like(hf), like(hi),
            pltpu.VMEM((3, time_filter.shape[0] // 2, LANE), F32),
            pltpu.VMEM((3, height_filter.shape[0] // 2, LANE), F32),
            t_buf, t_buf, t_buf, t_buf, h_buf, h_buf, h_buf, h_buf,
            pltpu.SemaphoreType.DMA((5,)),
            pltpu.SemaphoreType.DMA((1,)),
            pltpu.SemaphoreType.DMA((4, CHUNKS)),
            pltpu.SemaphoreType.DMA((4, CHUNKS)),
        ],
        compiler_params=pltpu.CompilerParams(collective_id=0, has_side_effects=True),
    )(frames_in, time_filter, height_filter, jnp.asarray(tf), jnp.asarray(ti), jnp.asarray(hf), jnp.asarray(hi))


def solution(mesh):
    return jax.shard_map(
        shards,
        mesh=mesh,
        in_specs=(P("tm", "height", None), P(), P()),
        out_specs=P("tm", "height", None),
        check_vma=False,
    )
```

time: 163 us -> 64 us (0.39)
  local copies, waits for them, and re-layouts: 81.2 us -> 4.68 us
  Pallas kernels: 0 us -> 59 us
  starting transfers between devices: 39.2 us -> 0 us
  waiting for transfers between devices: 19.8 us -> 0 us
  blocking collectives: 15.7 us -> 0 us
  matrix products: 5.71 us -> 0 us
    pallas_call x0 -> x1, Pallas kernels: none -> 59 us  [shards(): pl.pallas_call(functools.partial(kernel, tm_count, height_count), out_sha...]
    reshape x7 -> x0, local copies, waits for them, and re-layouts: 48.2 us -> none  [the longest x5 47.1 us: shifted_taps(): return flat.reshape(distinct, size, 2 * size - 1)[:, :, :size]]
    all_to_all x3 -> x0, starting transfers between devices: 39.2 us -> none  [the longest x1 17.1 us: shards(): lax.all_to_all(frames_in, 'tm', split_axis=2, concat_axis=0, tiled=True)]
    all_to_all x3 -> x0, waiting for transfers between devices: 19.8 us -> none  [the longest x1 19.8 us: shards(): lax.all_to_all(result, 'tm', split_axis=0, concat_axis=2, tiled=True)]
    all_to_all x1 -> x0, blocking collectives: 15.7 us -> none  [shards(): lax.all_to_all(result, 'height', split_axis=1, concat_axis=2, tiled=True)]
    unnamed x40 -> x3, local copies, waits for them, and re-layouts: 19.9 us -> 4.68 us
    slice x8 -> x0, local copies, waits for them, and re-layouts: 5.74 us -> none  [the longest x5 5.65 us: shifted_taps(): lax.slice_in_dim(repeated, size - 1, size - 1 + size * (2 * size - 1), ax...]
    dot_general x7 -> x0, matrix products: 5.71 us -> none  [the longest x1 2.77 us: row_convolve(): jnp.einsum('cab,cxfb->cxfa', circulant, arranged, preferred_element_type=...]
  transfers between devices with their start and end apart: 3 -> 0, of which waited for: 1 -> 0; matrix products, arithmetic and copies ran while one was open for 36% -> 0% of each run, Pallas kernels for 0% -> 0%
where the time goes in v1:
time: 64 us; the launch traced here: 63.7 us
  Pallas kernels  59 us (92%)
  local copies, waits for them, and re-layouts  4.68 us (7%)
    pallas_call x1, Pallas kernels, shards(): pl.pallas_call(functools.partial(kernel, tm_count, height_count), out_sha...  59 us
    unnamed x3, local copies, waits for them, and re-layouts  4.68 us

profile of v1, /device:TPU:1, one launch (start us, length us, event | category | flops | bytes accessed | tf_op | source)
XLA Modules:
  0.0 63.7 jit_solution(3246694350410896197)
XLA Ops:
  0.0 1.4 %copy.9.height_taps = bf16[128,64]{1,0:T(8,128)(2,1)} copy(bf16[128,64]{0,1:T(8,128)(2,1)} %param.9) | data formatting | bytes 32768 | tf_op args[2]
  1.4 1.6 %copy.8.time_taps = bf16[512,64]{1,0:T(8,128)(2,1)} copy(bf16[512,64]{0,1:T(8,128)(2,1)} %param.8) | data formatting | bytes 131072 | tf_op args[1]
  3.0 59.0 %shard_map.73 = bf16[16,8,1024]{2,1,0:T(8,128)(2,1)} custom-call(bf16[16,8,1024]{2,1,0:T(8,128)(2,1)} %frames_hbm.1, bf16[512,64]{1,0:T(8,128)(2,1)} %copy.8.time_taps, bf16[128,64]{1,0:T(8,128)(2,1)} %copy.9.height_taps, bf16[1024,512]{1,0:T(8,128)(2,1)} %constant.8.clone.tf_hbm, bf16[2,512,512]{2,1,0:T(8,128)(2,1)} %constant.9.clone.ti_hbm, ...), custom_call_target="tpu_custom_call" | custom-call | tf_op jit(solution)/shard_map/pallas_call | solution.py:233
  62.1 1.7 %copy.11 = bf16[16,8,1024]{2,1,0:T(8,128)(2,1)} copy(bf16[16,8,1024]{2,1,0:T(8,128)(2,1)} %shard_map.73) | data formatting | bytes 524288

commit v2 on v1

--- a/solution.py
+++ b/solution.py
@@ -52,10 +52,12 @@
 
 
 def store_response(forward, taps, response):
-    size, channels = taps.shape
+    channels, size = taps.shape
     half = size // 2
-    spread = one_hot((channels, LANE), lambda r, c: r == c % channels)
-    spectrum = forward_dft(forward, dot(taps[...], spread).astype(BF16))
+    spread = one_hot((LANE, channels), lambda r, c: c == r % channels)
+    wide = dot(spread, taps[...]).astype(BF16)
+    both = lax.dot_general(forward[...], wide, (((1,), (1,)), ((), ())), preferred_element_type=F32)
+    spectrum = both[:size] + both[size:]
     first = lax.broadcasted_iota(jnp.int32, (half, LANE), 0) == 0
     scale = jnp.where(first, 1.0 / size, 2.0 / size)
     cosine, sine = spectrum[:half] * scale, spectrum[half:] * scale
@@ -81,7 +83,7 @@
     out,
     frames, tf, ti, hf, hi, t_response, h_response,
     t_send, t_have, t_done, t_back, h_send, h_have, h_done, h_back,
-    load_sems, own_sems, send_sems, recv_sems,
+    load_sems, send_sems, recv_sems,
 ):
     frames_dev, rows_dev, lane_total = frames.shape
     width = lane_total // CHUNKS
@@ -95,7 +97,10 @@
     loads = [
         pltpu.make_async_copy(src, dst, load_sems.at[i])
         for i, (src, dst) in enumerate(
-            [(frames_hbm, frames), (tf_hbm, tf), (ti_hbm, ti), (hf_hbm, hf), (hi_hbm, hi)]
+            [
+                (frames_hbm, frames), (tf_hbm, tf), (ti_hbm, ti), (hf_hbm, hf), (hi_hbm, hi),
+                (frames_hbm.at[:, :, pl.ds(width, width)], h_send.at[1]),
+            ]
         )
     ]
     for load in loads:
@@ -118,14 +123,21 @@
 
     loads[0].wait()
     swap_in = one_hot((block, block), lambda r, c: c == (r % frames_dev) * rows_dev + r // frames_dev)
-    rows = frames[...].astype(F32).reshape(block, lane_total).astype(BF16)
-    turned = dot(swap_in, rows).astype(BF16)
-    for c in range(CHUNKS):
+    swap_back = one_hot((block, block), lambda r, c: c == (r % rows_dev) * frames_dev + r // rows_dev)
+
+    def rows_first(values, c):
+        flat = values.astype(F32).reshape(block, width).astype(BF16)
+        turned = dot(swap_in, flat).astype(BF16)
         for g in range(groups):
-            lo = c * width + g * LANE
-            t_send[c, g * rows_dev:(g + 1) * rows_dev] = turned[:, lo:lo + LANE].reshape(
+            t_send[c, g * rows_dev:(g + 1) * rows_dev] = turned[:, g * LANE:(g + 1) * LANE].reshape(
                 rows_dev, frames_dev, LANE
             )
+
+    def frames_first(c, g):
+        tile = t_back[c, g * rows_dev:(g + 1) * rows_dev].reshape(block, LANE)
+        return dot(swap_back, tile).reshape(frames_dev, rows_dev, LANE)
+
+    rows_first(frames[:, :, :width], 0)
 
     pl.semaphore_wait(barrier, tm_count + height_count - 2)
 
@@ -169,47 +181,50 @@
         sent = src.at[c, pl.ds(0, peers - 1)]
         pltpu.make_async_copy(sent, sent, send_sems.at[phase, c]).wait()
 
-    for c in range(CHUNKS):
-        exchange_tm(0, c, t_send, t_have)
-
-    for load in loads[1:]:
-        load.wait()
-    store_response(tf, time_taps, t_response)
-    store_response(hf, height_taps, h_response)
-
-    def time_stage(c, carry):
+    def time_stage(c):
         arrived(0, c, t_have)
         values = t_have[c].reshape(tm_count * frames_dev, LANE)
         result = filtered(tf, ti, t_response, values).astype(BF16)
         t_done[c] = result.reshape(tm_count, frames_dev, LANE)
         exchange_tm(1, c, t_done, t_back)
-        return carry
-
-    lax.fori_loop(0, CHUNKS, time_stage, 0)
-
-    swap_back = one_hot((block, block), lambda r, c: c == (r % rows_dev) * frames_dev + r // rows_dev)
-
-    def height_stage(c, carry):
-        arrived(1, c, t_back)
-        for g in range(groups):
-            tile = t_back[c, g * rows_dev:(g + 1) * rows_dev].reshape(block, LANE)
-            turned = dot(swap_back, tile).reshape(frames_dev, rows_dev, LANE)
-            h_send[c, :, :, g * LANE:(g + 1) * LANE] = turned.astype(BF16)
-        exchange_height(2, c, h_send, h_have)
+
+    def height_stage(c):
         arrived(2, c, h_have)
         values = h_have[c].astype(F32).reshape(height_count * rows_dev, width).astype(BF16)
         result = filtered(hf, hi, h_response, values)
         h_done[c] = result.reshape(height_count, rows_dev, width).astype(BF16)
         exchange_height(3, c, h_done, h_back)
-        return carry
-
-    lax.fori_loop(0, CHUNKS, height_stage, 0)
-
-    for c in range(CHUNKS):
-        arrived(3, c, h_back)
-        lanes = slice(c * width, (c + 1) * width)
-        total = frames[:, :, lanes].astype(F32) + h_back[c].astype(F32)
-        out[:, :, lanes] = total.astype(BF16)
+
+    exchange_tm(0, 0, t_send, t_have)
+    loads[5].wait()
+    exchange_height(2, 1, h_send, h_have)
+    for load in loads[1:5]:
+        load.wait()
+    store_response(hf, height_taps, h_response)
+    store_response(tf, time_taps, t_response)
+
+    height_stage(1)
+    time_stage(0)
+
+    arrived(3, 1, h_back)
+    rows_first(h_back[1], 1)
+    exchange_tm(0, 1, t_send, t_have)
+
+    arrived(1, 0, t_back)
+    for g in range(groups):
+        h_send[0, :, :, g * LANE:(g + 1) * LANE] = frames_first(0, g).astype(BF16)
+    exchange_height(2, 0, h_send, h_have)
+
+    time_stage(1)
+    height_stage(0)
+
+    arrived(3, 0, h_back)
+    out[:, :, :width] = (frames[:, :, :width].astype(F32) + h_back[0].astype(F32)).astype(BF16)
+
+    arrived(1, 1, t_back)
+    for g in range(groups):
+        lanes = slice(width + g * LANE, width + (g + 1) * LANE)
+        out[:, :, lanes] = (frames[:, :, lanes].astype(F32) + frames_first(1, g)).astype(BF16)
 
     for c in range(CHUNKS):
         departed(0, c, t_send, tm_count)
@@ -241,13 +256,12 @@
             pltpu.VMEM((3, time_filter.shape[0] // 2, LANE), F32),
             pltpu.VMEM((3, height_filter.shape[0] // 2, LANE), F32),
             t_buf, t_buf, t_buf, t_buf, h_buf, h_buf, h_buf, h_buf,
-            pltpu.SemaphoreType.DMA((5,)),
-            pltpu.SemaphoreType.DMA((1,)),
+            pltpu.SemaphoreType.DMA((6,)),
             pltpu.SemaphoreType.DMA((4, CHUNKS)),
             pltpu.SemaphoreType.DMA((4, CHUNKS)),
         ],
         compiler_params=pltpu.CompilerParams(collective_id=0, has_side_effects=True),
-    )(frames_in, time_filter, height_filter, jnp.asarray(tf), jnp.asarray(ti), jnp.asarray(hf), jnp.asarray(hi))
+    )(frames_in, time_filter.T, height_filter.T, jnp.asarray(tf), jnp.asarray(ti), jnp.asarray(hf), jnp.asarray(hi))
 
 
 def solution(mesh):

time: 64 us -> 53.6 us (0.84)
  Pallas kernels: 59 us -> 51.7 us
  local copies, waits for them, and re-layouts: 4.68 us -> 1.67 us
    pallas_call x1, Pallas kernels: 59 us -> 51.7 us  [shards(): pl.pallas_call(functools.partial(kernel, tm_count, height_count), out_sha...]
    unnamed x3 -> x1, local copies, waits for them, and re-layouts: 4.68 us -> 1.67 us
where the time goes in v2:
time: 53.6 us; the launch traced here: 53.4 us
  Pallas kernels  51.7 us (96%)
  local copies, waits for them, and re-layouts  1.67 us (3%)
    pallas_call x1, Pallas kernels, shards(): pl.pallas_call(functools.partial(kernel, tm_count, height_count), out_sha...  51.7 us
    unnamed x1, local copies, waits for them, and re-layouts  1.67 us

profile of v2, /device:TPU:1, one launch (start us, length us, event | category | flops | bytes accessed | tf_op | source)
XLA Modules:
  0.0 53.4 jit_solution(2241697353883338980)
XLA Ops:
  0.0 51.7 %shard_map.73 = bf16[16,8,1024]{2,1,0:T(8,128)(2,1)} custom-call(bf16[16,8,1024]{2,1,0:T(8,128)(2,1)} %frames_hbm.1, bf16[64,512]{1,0:T(8,128)(2,1)} %bitcast.2, bf16[64,128]{1,0:T(8,128)(2,1)} %bitcast.3, bf16[1024,512]{1,0:T(8,128)(2,1)} %constant.8.clone.tf_hbm, bf16[2,512,512]{2,1,0:T(8,128)(2,1)} %constant.9.clone.ti_hbm, ...), custom_call_target="tpu_custom_call" | custom-call | tf_op jit(solution)/shard_map/pallas_call | solution.py:248
  51.7 1.7 %copy.9 = bf16[16,8,1024]{2,1,0:T(8,128)(2,1)} copy(bf16[16,8,1024]{2,1,0:T(8,128)(2,1)} %shard_map.73) | data formatting | bytes 524288

commit v3 on v2

v3 whole, which is shorter than its diff:
```python
import functools

import jax
import jax.numpy as jnp
import numpy as np
from jax import lax
from jax.experimental import pallas as pl
from jax.experimental.pallas import tpu as pltpu
from jax.sharding import PartitionSpec as P

MESH = pl.DeviceIdType.MESH
F32, BF16 = jnp.float32, jnp.bfloat16
LANE = 128
CHUNKS = 2


def split(table):
    high = table.astype(np.float32).astype(jnp.bfloat16)
    low = (table - high.astype(np.float64)).astype(np.float32).astype(jnp.bfloat16)
    return high, low


def dft_rows(size):
    half = size // 2
    order = np.concatenate([np.arange(0, half, 2), np.arange(1, half, 2)])
    angle = 2.0 * np.pi * ((order[:, None] * np.arange(size)[None, :]) % size) / size
    sines = np.sin(angle)
    sines[0] = np.cos(np.pi * np.arange(size))
    return np.cos(angle), sines


def time_tables(size):
    half, quarter = size // 2, size // 4
    cosines, sines = dft_rows(size)
    parts = [
        np.concatenate([cosines[rows, :half], sines[rows, :half]], axis=0)
        for rows in (slice(0, quarter), slice(quarter, half))
    ]
    forward = np.concatenate(split(np.concatenate(parts, axis=0)), axis=0)
    inverse = np.stack([piece for part in parts for piece in split(part.T)])
    return forward, inverse


def height_tables(size):
    high, low = split(np.concatenate(dft_rows(size), axis=0))
    return np.concatenate([high, low], axis=1), np.concatenate([high.T, low.T], axis=1)


def dot(a, b):
    return jnp.dot(a, b, preferred_element_type=F32)


def halves(values):
    high = values.astype(BF16)
    return high, (values - high.astype(F32)).astype(BF16)


def one_hot(shape, hit):
    rows = lax.broadcasted_iota(jnp.int32, shape, 0)
    cols = lax.broadcasted_iota(jnp.int32, shape, 1)
    return jnp.where(hit(rows, cols), 1.0, 0.0).astype(BF16)


def time_forward(table, values):
    half, quarter = values.shape[0] // 2, values.shape[0] // 4
    both = dot(table[...], jnp.concatenate([values[:half], values[half:]], axis=1))
    both = both[:2 * half] + both[2 * half:]
    even = both[:half, :LANE] + both[:half, LANE:]
    odd = both[half:, :LANE] - both[half:, LANE:]
    cosine = jnp.concatenate([even[:quarter], odd[:quarter]], axis=0)
    sine = jnp.concatenate([even[quarter:], odd[quarter:]], axis=0)
    return cosine, sine


def time_inverse(table, cosine, sine):
    quarter = cosine.shape[0] // 2
    sums = []
    for p in range(2):
        rows = slice(p * quarter, (p + 1) * quarter)
        high, low = halves(jnp.concatenate([cosine[rows], sine[rows]], axis=0))
        main = dot(table[2 * p], jnp.concatenate([high, low], axis=1))
        sums.append(main[:, :LANE] + main[:, LANE:] + dot(table[2 * p + 1], high))
    return jnp.concatenate([sums[0] + sums[1], sums[0] - sums[1]], axis=0)


def height_forward(table, values):
    half = values.shape[0] // 2
    both = dot(table[...], jnp.concatenate([values, values], axis=0))
    return both[:half], both[half:]


def height_inverse(table, cosine, sine):
    high, low = halves(jnp.concatenate([cosine, sine], axis=0))
    return dot(table[...], jnp.concatenate([high, high], axis=0)) + dot(table[:, :high.shape[0]], low)


def store_response(forward, table, taps, response):
    channels, size = taps.shape
    spread = one_hot((LANE, channels), lambda r, c: c == r % channels)
    wide = jnp.transpose(dot(spread, taps[...])).astype(BF16)
    cosine, sine = forward(table, wide)
    first = lax.broadcasted_iota(jnp.int32, cosine.shape, 0) == 0
    scale = jnp.where(first, 1.0 / size, 2.0 / size)
    cosine, sine = cosine * scale, sine * scale
    response[0] = cosine
    response[1] = jnp.where(first, 0.0, sine)
    response[2] = jnp.where(first, sine, cosine)


def product(response, cosine, sine):
    wide = lambda which: jnp.concatenate([response[which]] * (cosine.shape[1] // LANE), axis=1)
    p, q, nyquist_p = wide(0), wide(1), wide(2)
    return cosine * p - sine * q, cosine * q + sine * nyquist_p


def kernel(
    tm_count, height_count,
    frames_hbm, time_taps, height_taps, tf_hbm, ti_hbm, hf_hbm, hi_hbm,
    out,
    frames, tf, ti, hf, hi, t_response, h_response,
    t_send, t_have, t_done, t_back, h_send, h_have, h_done, h_back,
    load_sems, send_sems, recv_sems,
):
    frames_dev, rows_dev, lane_total = frames.shape
    width = lane_total // CHUNKS
    groups = width // LANE
    block = frames_dev * rows_dev
    tm = lax.axis_index("tm")
    height = lax.axis_index("height")
    row_size = 4
    y_count = height_count // row_size

    loads = [
        pltpu.make_async_copy(src, dst, load_sems.at[i])
        for i, (src, dst) in enumerate(
            [
                (frames_hbm, frames), (tf_hbm, tf), (ti_hbm, ti), (hf_hbm, hf), (hi_hbm, hi),
                (frames_hbm.at[:, :, pl.ds(width, width)], h_send.at[1]),
            ]
        )
    ]
    for load in loads:
        load.start()

    barrier = pltpu.get_barrier_semaphore()

    def tm_peer(d):
        return lax.rem(tm + d, tm_count)

    def height_peer(i):
        k = lax.rem(lax.div(i, 2), y_count)
        away = y_count // 2 + lax.div(k + 1, 2) * (1 - 2 * lax.rem(k, 2))
        cross = lax.rem(lax.div(height, 2) + 1 - lax.div(i, 2 * y_count), 2)
        core = lax.rem(height + 1 - lax.rem(i, 2), 2)
        return lax.rem(lax.div(height, row_size) + away, y_count) * row_size + cross * 2 + core

    def each_tm(act):
        act(tm_peer(tm_count // 2))

        def pair(m, carry):
            act(tm_peer(tm_count // 2 - m))
            act(tm_peer(tm_count // 2 + m))
            return carry

        lax.fori_loop(1, tm_count // 2, pair, 0)

    def each_height(act):
        def one(i, carry):
            act(height_peer(i))
            return carry

        lax.fori_loop(0, height_count - 1, one, 0)

    each_tm(lambda peer: pl.semaphore_signal(barrier, inc=1, device_id=(peer, height), device_id_type=MESH))
    each_height(lambda peer: pl.semaphore_signal(barrier, inc=1, device_id=(tm, peer), device_id_type=MESH))

    loads[0].wait()
    swap_in = one_hot((block, block), lambda r, c: c == (r % frames_dev) * rows_dev + r // frames_dev)
    swap_back = one_hot((block, block), lambda r, c: c == (r % rows_dev) * frames_dev + r // rows_dev)

    def rows_first(values, c):
        flat = values.astype(F32).reshape(block, width).astype(BF16)
        turned = dot(swap_in, flat).astype(BF16)
        for g in range(groups):
            t_send[c, g * rows_dev:(g + 1) * rows_dev] = turned[:, g * LANE:(g + 1) * LANE].reshape(
                rows_dev, frames_dev, LANE
            )

    def frames_first(c, g):
        tile = t_back[c, g * rows_dev:(g + 1) * rows_dev].reshape(block, LANE)
        return dot(swap_back, tile).reshape(frames_dev, rows_dev, LANE)

    rows_first(frames[:, :, :width], 0)
    loads[5].wait()

    pl.semaphore_wait(barrier, tm_count + height_count - 2)

    def exchange_tm(phase, c, src, dst):
        each_tm(lambda peer: pltpu.make_async_remote_copy(
            src_ref=src.at[c, peer], dst_ref=dst.at[c, tm],
            send_sem=send_sems.at[phase, c], recv_sem=recv_sems.at[phase, c],
            device_id=(peer, height), device_id_type=MESH,
        ).start())
        pltpu.make_async_copy(src.at[c, tm], dst.at[c, tm], recv_sems.at[phase, c]).start()

    def exchange_height(phase, c, src, dst):
        each_height(lambda peer: pltpu.make_async_remote_copy(
            src_ref=src.at[c, peer], dst_ref=dst.at[c, height],
            send_sem=send_sems.at[phase, c], recv_sem=recv_sems.at[phase, c],
            device_id=(tm, peer), device_id_type=MESH,
        ).start())
        pltpu.make_async_copy(src.at[c, height], dst.at[c, height], recv_sems.at[phase, c]).start()

    def arrived(phase, c, dst):
        pltpu.make_async_copy(dst.at[c], dst.at[c], recv_sems.at[phase, c]).wait()

    def departed(phase, c, src, peers):
        sent = src.at[c, pl.ds(0, peers - 1)]
        pltpu.make_async_copy(sent, sent, send_sems.at[phase, c]).wait()

    def time_stage(c):
        arrived(0, c, t_have)
        values = t_have[c].reshape(tm_count * frames_dev, LANE)
        result = time_inverse(ti, *product(t_response, *time_forward(tf, values))).astype(BF16)
        t_done[c] = result.reshape(tm_count, frames_dev, LANE)
        exchange_tm(1, c, t_done, t_back)

    def height_stage(c):
        arrived(2, c, h_have)
        values = h_have[c].astype(F32).reshape(height_count * rows_dev, width).astype(BF16)
        result = height_inverse(hi, *product(h_response, *height_forward(hf, values)))
        h_done[c] = result.reshape(height_count, rows_dev, width).astype(BF16)
        exchange_height(3, c, h_done, h_back)

    exchange_height(2, 1, h_send, h_have)
    exchange_tm(0, 0, t_send, t_have)
    for load in loads[1:5]:
        load.wait()
    store_response(height_forward, hf, height_taps, h_response)
    store_response(time_forward, tf, time_taps, t_response)

    height_stage(1)
    time_stage(0)

    arrived(3, 1, h_back)
    rows_first(h_back[1], 1)
    exchange_tm(0, 1, t_send, t_have)

    arrived(1, 0, t_back)
    for g in range(groups):
        h_send[0, :, :, g * LANE:(g + 1) * LANE] = frames_first(0, g).astype(BF16)
    exchange_height(2, 0, h_send, h_have)

    time_stage(1)
    height_stage(0)

    arrived(3, 0, h_back)
    out[:, :, :width] = (frames[:, :, :width].astype(F32) + h_back[0].astype(F32)).astype(BF16)

    arrived(1, 1, t_back)
    for g in range(groups):
        lanes = slice(width + g * LANE, width + (g + 1) * LANE)
        out[:, :, lanes] = (frames[:, :, lanes].astype(F32) + frames_first(1, g)).astype(BF16)

    for c in range(CHUNKS):
        departed(0, c, t_send, tm_count)
        departed(1, c, t_done, tm_count)
        departed(2, c, h_send, height_count)
        departed(3, c, h_done, height_count)


def shards(frames_in, time_filter, height_filter):
    frames_dev, rows_dev, lane_total = frames_in.shape
    tm_count = lax.axis_size("tm")
    height_count = lax.axis_size("height")
    width = lane_total // CHUNKS
    tf, ti = time_tables(time_filter.shape[0])
    hf, hi = height_tables(height_filter.shape[0])
    t_buf = pltpu.VMEM((CHUNKS, tm_count, frames_dev, LANE), BF16)
    h_buf = pltpu.VMEM((CHUNKS, height_count, rows_dev, width), BF16)
    like = lambda a: pltpu.VMEM(a.shape, BF16)
    hbm = pl.BlockSpec(memory_space=pl.ANY)
    vmem = pl.BlockSpec(memory_space=pltpu.VMEM)
    return pl.pallas_call(
        functools.partial(kernel, tm_count, height_count),
        out_shape=jax.ShapeDtypeStruct(frames_in.shape, BF16),
        in_specs=[hbm, vmem, vmem, hbm, hbm, hbm, hbm],
        out_specs=vmem,
        scratch_shapes=[
            pltpu.VMEM(frames_in.shape, BF16),
            like(tf), like(ti), like(hf), like(hi),
            pltpu.VMEM((3, time_filter.shape[0] // 2, LANE), F32),
            pltpu.VMEM((3, height_filter.shape[0] // 2, LANE), F32),
            t_buf, t_buf, t_buf, t_buf, h_buf, h_buf, h_buf, h_buf,
            pltpu.SemaphoreType.DMA((6,)),
            pltpu.SemaphoreType.DMA((4, CHUNKS)),
            pltpu.SemaphoreType.DMA((4, CHUNKS)),
        ],
        compiler_params=pltpu.CompilerParams(collective_id=0, has_side_effects=True),
    )(frames_in, time_filter.T, height_filter.T, jnp.asarray(tf), jnp.asarray(ti), jnp.asarray(hf), jnp.asarray(hi))


def solution(mesh):
    return jax.shard_map(
        shards,
        mesh=mesh,
        in_specs=(P("tm", "height", None), P(), P()),
        out_specs=P("tm", "height", None),
        check_vma=False,
    )
```

time: 53.6 us -> 51.8 us (0.966)
  Pallas kernels: 51.7 us -> 49.9 us
    pallas_call x1, Pallas kernels: 51.7 us -> 49.9 us  [shards(): pl.pallas_call(functools.partial(kernel, tm_count, height_count), out_sha...]
where the time goes in v3:
time: 51.8 us; the launch traced here: 51.6 us
  Pallas kernels  49.9 us (96%)
  local copies, waits for them, and re-layouts  1.67 us (3%)
    pallas_call x1, Pallas kernels, shards(): pl.pallas_call(functools.partial(kernel, tm_count, height_count), out_sha...  49.9 us
    unnamed x1, local copies, waits for them, and re-layouts  1.67 us

profile of v3, /device:TPU:1, one launch (start us, length us, event | category | flops | bytes accessed | tf_op | source)
XLA Modules:
  0.0 51.6 jit_solution(3514367466303641736)
XLA Ops:
  0.0 49.9 %shard_map.73 = bf16[16,8,1024]{2,1,0:T(8,128)(2,1)} custom-call(bf16[16,8,1024]{2,1,0:T(8,128)(2,1)} %frames_hbm.1, bf16[64,512]{1,0:T(8,128)(2,1)} %bitcast.2, bf16[64,128]{1,0:T(8,128)(2,1)} %bitcast.3, bf16[1024,256]{1,0:T(8,128)(2,1)} %constant.8.clone.tf_hbm, bf16[4,256,256]{2,1,0:T(8,128)(2,1)} %constant.9.clone.ti_hbm, ...), custom_call_target="tpu_custom_call" | custom-call | tf_op jit(solution)/shard_map/pallas_call | solution.py:284
  49.9 1.7 %copy.9 = bf16[16,8,1024]{2,1,0:T(8,128)(2,1)} copy(bf16[16,8,1024]{2,1,0:T(8,128)(2,1)} %shard_map.73) | data formatting | bytes 524288

commit v4 on v3

--- a/solution.py
+++ b/solution.py
@@ -115,9 +115,9 @@
 
 def kernel(
     tm_count, height_count,
-    frames_hbm, time_taps, height_taps, tf_hbm, ti_hbm, hf_hbm, hi_hbm,
+    frames_hbm, tt_hbm, ht_hbm, tf_hbm, ti_hbm, hf_hbm, hi_hbm,
     out,
-    frames, tf, ti, hf, hi, t_response, h_response,
+    frames, time_taps, height_taps, tf, ti, hf, hi, t_response, h_response,
     t_send, t_have, t_done, t_back, h_send, h_have, h_done, h_back,
     load_sems, send_sems, recv_sems,
 ):
@@ -127,32 +127,18 @@
     block = frames_dev * rows_dev
     tm = lax.axis_index("tm")
     height = lax.axis_index("height")
-    row_size = 4
-    y_count = height_count // row_size
-
-    loads = [
-        pltpu.make_async_copy(src, dst, load_sems.at[i])
-        for i, (src, dst) in enumerate(
-            [
-                (frames_hbm, frames), (tf_hbm, tf), (ti_hbm, ti), (hf_hbm, hf), (hi_hbm, hi),
-                (frames_hbm.at[:, :, pl.ds(width, width)], h_send.at[1]),
-            ]
-        )
-    ]
-    for load in loads:
-        load.start()
 
     barrier = pltpu.get_barrier_semaphore()
 
     def tm_peer(d):
         return lax.rem(tm + d, tm_count)
 
-    def height_peer(i):
-        k = lax.rem(lax.div(i, 2), y_count)
-        away = y_count // 2 + lax.div(k + 1, 2) * (1 - 2 * lax.rem(k, 2))
-        cross = lax.rem(lax.div(height, 2) + 1 - lax.div(i, 2 * y_count), 2)
-        core = lax.rem(height + 1 - lax.rem(i, 2), 2)
-        return lax.rem(lax.div(height, row_size) + away, y_count) * row_size + cross * 2 + core
+    row, column, core = lax.div(height, 4), lax.rem(lax.div(height, 2), 2), lax.rem(height, 2)
+    y_count = height_count // 4
+    rows_at = [lax.rem(row + away, y_count) * 4 for away in range(y_count)]
+    pairs_at = [(lax.rem(column + x, 2)) * 2 + lax.rem(core + c, 2) for x in (1, 0) for c in (1, 0)]
+    by_hops = sorted(range(y_count), key=lambda away: -min(away, y_count - away))
+    height_peers = [rows_at[y] + pairs_at[2 * x + c] for x in (0, 1) for y in by_hops for c in (0, 1)][:-1]
 
     def each_tm(act):
         act(tm_peer(tm_count // 2))
@@ -165,14 +151,21 @@
         lax.fori_loop(1, tm_count // 2, pair, 0)
 
     def each_height(act):
-        def one(i, carry):
-            act(height_peer(i))
-            return carry
-
-        lax.fori_loop(0, height_count - 1, one, 0)
+        for peer in height_peers:
+            act(peer)
 
     each_tm(lambda peer: pl.semaphore_signal(barrier, inc=1, device_id=(peer, height), device_id_type=MESH))
     each_height(lambda peer: pl.semaphore_signal(barrier, inc=1, device_id=(tm, peer), device_id_type=MESH))
+
+    loads = [
+        pltpu.make_async_copy(src, dst, load_sems.at[i])
+        for i, (src, dst) in enumerate([
+            (frames_hbm, frames), (frames_hbm.at[:, :, pl.ds(width, width)], h_send.at[1]),
+            (ht_hbm, height_taps), (hf_hbm, hf), (tt_hbm, time_taps), (tf_hbm, tf), (hi_hbm, hi), (ti_hbm, ti),
+        ])
+    ]
+    for load in loads:
+        load.start()
 
     loads[0].wait()
     swap_in = one_hot((block, block), lambda r, c: c == (r % frames_dev) * rows_dev + r // frames_dev)
@@ -191,7 +184,7 @@
         return dot(swap_back, tile).reshape(frames_dev, rows_dev, LANE)
 
     rows_first(frames[:, :, :width], 0)
-    loads[5].wait()
+    loads[1].wait()
 
     pl.semaphore_wait(barrier, tm_count + height_count - 2)
 
@@ -234,7 +227,7 @@
 
     exchange_height(2, 1, h_send, h_have)
     exchange_tm(0, 0, t_send, t_have)
-    for load in loads[1:5]:
+    for load in loads[2:]:
         load.wait()
     store_response(height_forward, hf, height_taps, h_response)
     store_response(time_forward, tf, time_taps, t_response)
@@ -279,20 +272,20 @@
     t_buf = pltpu.VMEM((CHUNKS, tm_count, frames_dev, LANE), BF16)
     h_buf = pltpu.VMEM((CHUNKS, height_count, rows_dev, width), BF16)
     like = lambda a: pltpu.VMEM(a.shape, BF16)
-    hbm = pl.BlockSpec(memory_space=pl.ANY)
+    hbm = pl.BlockSpec(memory_space=pltpu.MemorySpace.HBM)
     vmem = pl.BlockSpec(memory_space=pltpu.VMEM)
     return pl.pallas_call(
         functools.partial(kernel, tm_count, height_count),
-        out_shape=jax.ShapeDtypeStruct(frames_in.shape, BF16),
-        in_specs=[hbm, vmem, vmem, hbm, hbm, hbm, hbm],
+        out_shape=pltpu.VMEM(frames_in.shape, BF16),
+        in_specs=[hbm] * 7,
         out_specs=vmem,
         scratch_shapes=[
             pltpu.VMEM(frames_in.shape, BF16),
-            like(tf), like(ti), like(hf), like(hi),
+            like(time_filter.T), like(height_filter.T), like(tf), like(ti), like(hf), like(hi),
             pltpu.VMEM((3, time_filter.shape[0] // 2, LANE), F32),
             pltpu.VMEM((3, height_filter.shape[0] // 2, LANE), F32),
             t_buf, t_buf, t_buf, t_buf, h_buf, h_buf, h_buf, h_buf,
-            pltpu.SemaphoreType.DMA((6,)),
+            pltpu.SemaphoreType.DMA((8,)),
             pltpu.SemaphoreType.DMA((4, CHUNKS)),
             pltpu.SemaphoreType.DMA((4, CHUNKS)),
         ],

time: 51.8 us -> 49.2 us (0.950)
  Pallas kernels: 49.9 us -> 48.3 us
  local copies, waits for them, and re-layouts: 1.67 us -> 0.71 us
    pallas_call x1, Pallas kernels: 49.9 us -> 48.3 us  [shards(): pl.pallas_call(functools.partial(kernel, tm_count, height_count), out_sha...]
    unnamed x1, local copies, waits for them, and re-layouts: 1.67 us -> 0.71 us
where the time goes in v4:
time: 49.2 us; the launch traced here: 49 us
  Pallas kernels  48.3 us (98%)
  local copies, waits for them, and re-layouts  0.71 us (1%)
    pallas_call x1, Pallas kernels, shards(): pl.pallas_call(functools.partial(kernel, tm_count, height_count), out_sha...  48.3 us

profile of v4, /device:TPU:1, one launch (start us, length us, event | category | flops | bytes accessed | tf_op | source)
XLA Modules:
  0.0 49.0 jit_solution(15656162926371391181)
XLA Ops:
  0.0 48.3 %shard_map.73 = bf16[16,8,1024]{2,1,0:T(8,128)(2,1)S(1)} custom-call(bf16[16,8,1024]{2,1,0:T(8,128)(2,1)} %frames_hbm.1, bf16[64,512]{1,0:T(8,128)(2,1)} %bitcast.2, bf16[64,128]{1,0:T(8,128)(2,1)} %bitcast.3, bf16[1024,256]{1,0:T(8,128)(2,1)} %constant.8.clone.tf_hbm, bf16[4,256,256]{2,1,0:T(8,128)(2,1)} %constant.9.clone.ti_hbm, ...), custom_call_target="tpu_custom_call" | custom-call | tf_op jit(solution)/shard_map/pallas_call | solution.py:277
  48.3 0.7 %copy.9 = bf16[16,8,1024]{2,1,0:T(8,128)(2,1)} copy(bf16[16,8,1024]{2,1,0:T(8,128)(2,1)S(1)} %shard_map.73) | data formatting | bytes 524288

commit v5 on v4

--- a/solution.py
+++ b/solution.py
@@ -12,6 +12,7 @@
 F32, BF16 = jnp.float32, jnp.bfloat16
 LANE = 128
 CHUNKS = 2
+EARLY_PLANES = 8
 
 
 def split(table):
@@ -36,7 +37,7 @@
         np.concatenate([cosines[rows, :half], sines[rows, :half]], axis=0)
         for rows in (slice(0, quarter), slice(quarter, half))
     ]
-    forward = np.concatenate(split(np.concatenate(parts, axis=0)), axis=0)
+    forward = np.concatenate(split(np.concatenate(parts, axis=0)), axis=1)
     inverse = np.stack([piece for part in parts for piece in split(part.T)])
     return forward, inverse
 
@@ -63,8 +64,8 @@
 
 def time_forward(table, values):
     half, quarter = values.shape[0] // 2, values.shape[0] // 4
-    both = dot(table[...], jnp.concatenate([values[:half], values[half:]], axis=1))
-    both = both[:2 * half] + both[2 * half:]
+    pair = jnp.concatenate([values[:half], values[half:]], axis=1)
+    both = dot(table[...], jnp.concatenate([pair, pair], axis=0))
     even = both[:half, :LANE] + both[:half, LANE:]
     odd = both[half:, :LANE] - both[half:, LANE:]
     cosine = jnp.concatenate([even[:quarter], odd[:quarter]], axis=0)
@@ -196,6 +197,23 @@
         ).start())
         pltpu.make_async_copy(src.at[c, tm], dst.at[c, tm], recv_sems.at[phase, c]).start()
 
+    def from_home(c, first, last):
+        def send(peer, carry):
+            @pl.when(peer != tm)
+            def _():
+                pltpu.make_async_remote_copy(
+                    src_ref=t_done.at[c, peer], dst_ref=t_back.at[c, tm],
+                    send_sem=send_sems.at[1, c], recv_sem=recv_sems.at[1, c],
+                    device_id=(peer, height), device_id_type=MESH,
+                ).start()
+
+            return carry
+
+        lax.fori_loop(first, last, send, 0)
+
+    def own_frames(c):
+        pltpu.make_async_copy(t_done.at[c, tm], t_back.at[c, tm], recv_sems.at[1, c]).start()
+
     def exchange_height(phase, c, src, dst):
         each_height(lambda peer: pltpu.make_async_remote_copy(
             src_ref=src.at[c, peer], dst_ref=dst.at[c, height],
@@ -216,7 +234,7 @@
         values = t_have[c].reshape(tm_count * frames_dev, LANE)
         result = time_inverse(ti, *product(t_response, *time_forward(tf, values))).astype(BF16)
         t_done[c] = result.reshape(tm_count, frames_dev, LANE)
-        exchange_tm(1, c, t_done, t_back)
+        own_frames(c)
 
     def height_stage(c):
         arrived(2, c, h_have)
@@ -232,19 +250,34 @@
     store_response(height_forward, hf, height_taps, h_response)
     store_response(time_forward, tf, time_taps, t_response)
 
+    early = EARLY_PLANES * 2
+
+    def turn_to_height():
+        arrived(1, 0, t_back)
+        for g in range(groups):
+            h_send[0, :, :, g * LANE:(g + 1) * LANE] = frames_first(0, g).astype(BF16)
+        exchange_height(2, 0, h_send, h_have)
+
     height_stage(1)
     time_stage(0)
+    from_home(0, 0, early)
 
     arrived(3, 1, h_back)
     rows_first(h_back[1], 1)
     exchange_tm(0, 1, t_send, t_have)
-
-    arrived(1, 0, t_back)
-    for g in range(groups):
-        h_send[0, :, :, g * LANE:(g + 1) * LANE] = frames_first(0, g).astype(BF16)
-    exchange_height(2, 0, h_send, h_have)
+    from_home(0, early, tm_count)
+
+    @pl.when(tm < early)
+    def _():
+        turn_to_height()
 
     time_stage(1)
+    from_home(1, 0, tm_count)
+
+    @pl.when(tm >= early)
+    def _():
+        turn_to_height()
+
     height_stage(0)
 
     arrived(3, 0, h_back)

time: 49.2 us -> 48.2 us (0.980)
  Pallas kernels: 48.3 us -> 47.4 us
    pallas_call x1, Pallas kernels: 48.3 us -> 47.4 us  [shards(): pl.pallas_call(functools.partial(kernel, tm_count, height_count), out_sha...]
where the time goes in v5:
time: 48.2 us; the launch traced here: 48.1 us
  Pallas kernels  47.4 us (98%)
  local copies, waits for them, and re-layouts  0.71 us (1%)
    pallas_call x1, Pallas kernels, shards(): pl.pallas_call(functools.partial(kernel, tm_count, height_count), out_sha...  47.4 us

profile of v5, /device:TPU:1, one launch (start us, length us, event | category | flops | bytes accessed | tf_op | source)
XLA Modules:
  0.0 48.1 jit_solution(2831205369788758372)
XLA Ops:
  0.0 47.4 %shard_map.73 = bf16[16,8,1024]{2,1,0:T(8,128)(2,1)S(1)} custom-call(bf16[16,8,1024]{2,1,0:T(8,128)(2,1)} %frames_hbm.1, bf16[64,512]{1,0:T(8,128)(2,1)} %bitcast.2, bf16[64,128]{1,0:T(8,128)(2,1)} %bitcast.3, bf16[512,512]{1,0:T(8,128)(2,1)} %constant.8.clone.tf_hbm, bf16[4,256,256]{2,1,0:T(8,128)(2,1)} %constant.9.clone.ti_hbm, ...), custom_call_target="tpu_custom_call" | custom-call | tf_op jit(solution)/shard_map/pallas_call | solution.py:310
  47.4 0.7 %copy.9 = bf16[16,8,1024]{2,1,0:T(8,128)(2,1)} copy(bf16[16,8,1024]{2,1,0:T(8,128)(2,1)S(1)} %shard_map.73) | data formatting | bytes 524288

commit v6 on v5

--- a/solution.py
+++ b/solution.py
@@ -271,6 +271,12 @@
     def _():
         turn_to_height()
 
+    height_first = jnp.logical_and(tm < 2, core == 0)
+
+    @pl.when(height_first)
+    def _():
+        height_stage(0)
+
     time_stage(1)
     from_home(1, 0, tm_count)
 
@@ -278,7 +284,9 @@
     def _():
         turn_to_height()
 
-    height_stage(0)
+    @pl.when(jnp.logical_not(height_first))
+    def _():
+        height_stage(0)
 
     arrived(3, 0, h_back)
     out[:, :, :width] = (frames[:, :, :width].astype(F32) + h_back[0].astype(F32)).astype(BF16)

time: 48.2 us -> 47.6 us (0.988)
  Pallas kernels: 47.4 us -> 46.3 us
    pallas_call x1, Pallas kernels: 47.4 us -> 46.3 us  [shards(): pl.pallas_call(functools.partial(kernel, tm_count, height_count), out_sha...]
where the time goes in v6:
time: 47.6 us; the launch traced here: 47 us
  Pallas kernels  46.3 us (97%)
  local copies, waits for them, and re-layouts  0.71 us (1%)
    pallas_call x1, Pallas kernels, shards(): pl.pallas_call(functools.partial(kernel, tm_count, height_count), out_sha...  46.3 us

profile of v6, /device:TPU:1, one launch (start us, length us, event | category | flops | bytes accessed | tf_op | source)
XLA Modules:
  0.0 47.0 jit_solution(12471815923585874803)
XLA Ops:
  0.0 46.3 %shard_map.73 = bf16[16,8,1024]{2,1,0:T(8,128)(2,1)S(1)} custom-call(bf16[16,8,1024]{2,1,0:T(8,128)(2,1)} %frames_hbm.1, bf16[64,512]{1,0:T(8,128)(2,1)} %bitcast.2, bf16[64,128]{1,0:T(8,128)(2,1)} %bitcast.3, bf16[512,512]{1,0:T(8,128)(2,1)} %constant.8.clone.tf_hbm, bf16[4,256,256]{2,1,0:T(8,128)(2,1)} %constant.9.clone.ti_hbm, ...), custom_call_target="tpu_custom_call" | custom-call | tf_op jit(solution)/shard_map/pallas_call | solution.py:318
  46.3 0.7 %copy.9 = bf16[16,8,1024]{2,1,0:T(8,128)(2,1)} copy(bf16[16,8,1024]{2,1,0:T(8,128)(2,1)S(1)} %shard_map.73) | data formatting | bytes 524288

commit v7 on v6

--- a/solution.py
+++ b/solution.py
@@ -243,8 +243,8 @@
         h_done[c] = result.reshape(height_count, rows_dev, width).astype(BF16)
         exchange_height(3, c, h_done, h_back)
 
+    exchange_tm(0, 0, t_send, t_have)
     exchange_height(2, 1, h_send, h_have)
-    exchange_tm(0, 0, t_send, t_have)
     for load in loads[2:]:
         load.wait()
     store_response(height_forward, hf, height_taps, h_response)

time: 47.6 us -> 47.8 us (level)
  the two profiles are of different devices: /device:TPU:1 before, /device:TPU:10 now
where the time goes in v7:
time: 47.8 us; the launch traced here: 47.7 us
  Pallas kernels  47 us (98%)
  local copies, waits for them, and re-layouts  0.71 us (1%)
    pallas_call x1, Pallas kernels, shards(): pl.pallas_call(functools.partial(kernel, tm_count, height_count), out_sha...  47 us

profile of v7, /device:TPU:10, one launch (start us, length us, event | category | flops | bytes accessed | tf_op | source)
XLA Modules:
  0.0 47.7 jit_solution(10918324882152963539)
XLA Ops:
  0.0 47.0 %shard_map.73 = bf16[16,8,1024]{2,1,0:T(8,128)(2,1)S(1)} custom-call(bf16[16,8,1024]{2,1,0:T(8,128)(2,1)} %frames_hbm.1, bf16[64,512]{1,0:T(8,128)(2,1)} %bitcast.2, bf16[64,128]{1,0:T(8,128)(2,1)} %bitcast.3, bf16[512,512]{1,0:T(8,128)(2,1)} %constant.8.clone.tf_hbm, bf16[4,256,256]{2,1,0:T(8,128)(2,1)} %constant.9.clone.ti_hbm, ...), custom_call_target="tpu_custom_call" | custom-call | tf_op jit(solution)/shard_map/pallas_call | solution.py:318
  47.0 0.7 %copy.9 = bf16[16,8,1024]{2,1,0:T(8,128)(2,1)} copy(bf16[16,8,1024]{2,1,0:T(8,128)(2,1)S(1)} %shard_map.73) | data formatting | bytes 524288
